TPU v7x, 32 devices: a whole 2x2x4 slice. The times are simulated.
32 devices in a mesh: dp: 8 (over y, x, core), tensor: 4 (over z).
Axes of the slice: x: 2, y: 2, z: 4, core: 2. Of those that a mesh axis runs over, the one named last changes fastest.
Arguments:
- tokens: bfloat16 [16, 1024, 1024], P('dp', 'tensor'), may hold values from -6 to 6
- segments: int32 [16, 1024], P('dp'), may hold values from 0 to 3, as said below
- qkv_weight: bfloat16 [3, 1024, 1024], P(None, None, 'tensor'), may hold values from -0.1875 to 0.1875
- qkv_bias: float32 [3, 1024], P(None, 'tensor'), may hold values from -1.5 to 1.5
- out_weight: bfloat16 [1024, 1024], P('tensor'), may hold values from -0.75 to 0.75
- out_bias: float32 [1024], replicated, may hold values from -1.5 to 1.5
- gain_one: float32 [1024], replicated, may hold values from 0.5 to 1.5
- shift_one: float32 [1024], replicated, may hold values from -1.5 to 1.5
- up_weight: bfloat16 [1024, 4096], P(None, 'tensor'), may hold values from -0.1875 to 0.1875
- up_bias: float32 [4096], P('tensor'), may hold values from -1.5 to 1.5
- down_weight: bfloat16 [4096, 1024], P('tensor'), may hold values from -0.1875 to 0.1875
- down_bias: float32 [1024], replicated, may hold values from -1.5 to 1.5
- gain_two: float32 [1024], replicated, may hold values from 0.5 to 1.5
- shift_two: float32 [1024], replicated, may hold values from -1.5 to 1.5
- proj_weight: bfloat16 [1024, 288], replicated, may hold values from -0.1875 to 0.1875
- out_grad: bfloat16 [16, 1024, 1024], P('dp', 'tensor'), may hold values from -6 to 6
- embed_grad: bfloat16 [16, 1024, 288], P('dp', 'tensor'), may hold values from -6 to 6
Outputs:
- layer_out: bfloat16 [16, 1024, 1024], P('dp', 'tensor')
- embeddings: bfloat16 [16, 1024, 288], P('dp', 'tensor')
- tokens_grad: float32 [16, 1024, 1024], P('dp', 'tensor')
- qkv_weight_grad: float32 [3, 1024, 1024], P(None, None, 'tensor')
- qkv_bias_grad: float32 [3, 1024], P(None, 'tensor')
- out_weight_grad: float32 [1024, 1024], P('tensor')
- out_bias_grad: float32 [1024], replicated
- gain_one_grad: float32 [1024], replicated
- shift_one_grad: float32 [1024], replicated
- up_weight_grad: float32 [1024, 4096], P(None, 'tensor')
- up_bias_grad: float32 [4096], P('tensor')
- down_weight_grad: float32 [4096, 1024], P('tensor')
- down_bias_grad: float32 [1024], replicated
- gain_two_grad: float32 [1024], replicated
- shift_two_grad: float32 [1024], replicated
- proj_weight_grad: float32 [1024, 288], replicated
Inputs may be any that keep to these rules, and one draw needn't show every extreme that they name: `segments`: segment numbers never fall along a sequence; every sequence holds 4 documents, each of at least 200 tokens, and in every sequence some document has exactly 200.
All inputs are finite; a program needn't handle non-finite values.
Results may differ from a plain program's by a relative error of at most 0.018.
Values may be sent and summed in bfloat16 or wider, within the bound.
A program may use at most 192 MiB of HBM per device.

v0:
```python
import math
import jax
import jax.numpy as jnp
from jax import lax
from jax.sharding import PartitionSpec as P

HEAD_DIM = 64
eps = 1e-05


def as_sent(array):

    def short(part):
        return part.astype(jnp.bfloat16) if part.dtype == jnp.float32 else part

    return jax.tree.map(short, array)


def doc_positions(segment_rows):
    length = segment_rows.shape[-1]
    row_index = jnp.broadcast_to(jnp.arange(length, dtype=jnp.int32), segment_rows.shape)
    change = jnp.concatenate(
        [
            jnp.ones(segment_rows.shape[:-1] + (1,), jnp.bool_),
            segment_rows[..., 1:] != segment_rows[..., :-1],
        ],
        axis=-1,
    )
    doc_start = lax.cummax(
        jnp.where(change, row_index, jnp.zeros_like(row_index)), axis=segment_rows.ndim - 1
    )
    return row_index - doc_start


def rotary_tables(positions, head_dim):
    half_dim = head_dim // 2
    exponent = jnp.arange(half_dim, dtype=jnp.float32) * (2.0 / head_dim)
    frequency = jnp.exp(-exponent * math.log(10000.0))
    angles = positions.astype(jnp.float32)[..., None] * frequency
    angles = jnp.concatenate([angles, angles], axis=-1)
    return (jnp.cos(angles), jnp.sin(angles))


def rotate(field, cosine, sine):
    half_dim = field.shape[-1] // 2
    rotated = jnp.concatenate([-field[..., half_dim:], field[..., :half_dim]], axis=-1)
    return field * cosine + rotated * sine


def rotate_back(field, cosine, sine):
    half_dim = field.shape[-1] // 2
    rotated = jnp.concatenate([-field[..., half_dim:], field[..., :half_dim]], axis=-1)
    return field * cosine - rotated * sine


def norm_forward(field, gain, shift):
    row_mean = jnp.mean(field, axis=-1, keepdims=True)
    centred = field - row_mean
    variance = jnp.mean(centred * centred, axis=-1, keepdims=True)
    inv_std = lax.rsqrt(variance + eps)
    scaled = centred * inv_std
    return (scaled * gain + shift, scaled, inv_std)


def norm_backward(upstream, scaled, inv_std, gain):
    grad_scaled = upstream * gain
    grad_input = inv_std * (
        grad_scaled
        - jnp.mean(grad_scaled, axis=-1, keepdims=True)
        - scaled * jnp.mean(grad_scaled * scaled, axis=-1, keepdims=True)
    )
    return (grad_input, jnp.sum(upstream * scaled, axis=(0, 1)), jnp.sum(upstream, axis=(0, 1)))


def device_rows(full_rows, row_count):
    groups, length, model_width = full_rows.shape
    local_rows = length // lax.axis_size("tensor")
    blocks = row_count // (groups * local_rows)
    picked = full_rows
    picked = picked.reshape(groups, blocks, local_rows, model_width).transpose(1, 0, 2, 3)
    return picked.reshape(row_count, model_width)


def masked_scores(queries, keys, seg_row):
    scores = jnp.einsum("hqd,hkd->hqk", queries, keys, preferred_element_type=jnp.float32)
    same_doc = seg_row[:, None] == seg_row[None, :]
    return jnp.where(same_doc[None], scores, -1000000000.0)


def attend(inputs):
    queries, keys, values_low, seg_row = inputs
    scores = masked_scores(queries, keys, seg_row)
    row_peak = jnp.max(scores, axis=-1, keepdims=True)
    shifted = jnp.exp(scores - row_peak)
    row_total = jnp.sum(shifted, axis=-1, keepdims=True)
    probs = (shifted / row_total).astype(jnp.bfloat16)
    mixed_heads = jnp.einsum("hqk,hkd->hqd", probs, values_low, preferred_element_type=jnp.float32)
    return (mixed_heads, row_peak + jnp.log(row_total))


def attend_back(inputs):
    queries, keys, values_low, seg_row, log_total, grad_mixed = inputs
    scores = masked_scores(queries, keys, seg_row)
    probs = jnp.exp(scores - log_total)
    grad_values = jnp.einsum(
        "hqk,hqd->hkd", probs.astype(jnp.bfloat16), grad_mixed, preferred_element_type=jnp.float32
    )
    grad_probs = jnp.einsum(
        "hqd,hkd->hqk", grad_mixed, values_low, preferred_element_type=jnp.float32
    )
    row_inner = jnp.sum(probs * grad_probs, axis=-1, keepdims=True)
    grad_scores = (probs * (grad_probs - row_inner)).astype(jnp.bfloat16)
    grad_queries = jnp.einsum("hqk,hkd->hqd", grad_scores, keys, preferred_element_type=jnp.float32)
    grad_keys = jnp.einsum("hqk,hqd->hkd", grad_scores, queries, preferred_element_type=jnp.float32)
    return (grad_queries, grad_keys, grad_values)


def process(tokens, segments, out_grad, embed_grad, weights):
    (
        qkv_weight,
        qkv_bias,
        out_weight,
        out_bias,
        gain_one,
        shift_one,
        up_weight,
        up_bias,
        down_weight,
        down_bias,
        gain_two,
        shift_two,
        proj_weight,
    ) = weights
    groups, local_rows, model_width = tokens.shape
    length = segments.shape[1]
    heads_here = qkv_weight.shape[2] // HEAD_DIM
    q_scale = HEAD_DIM ** (-0.5)
    cosine, sine = rotary_tables(doc_positions(segments), HEAD_DIM)
    cosine = cosine[:, None]
    sine = sine[:, None]

    def split_heads(field):
        return field.reshape(groups, length, heads_here, HEAD_DIM).transpose(0, 2, 1, 3)

    def join_heads(field):
        return field.transpose(0, 2, 1, 3).reshape(groups, length, heads_here * HEAD_DIM)

    whole_tokens = lax.all_gather(tokens, "tensor", axis=1, tiled=True)
    projected = jnp.einsum(
        "gld,cde->cgle", whole_tokens, qkv_weight, preferred_element_type=jnp.float32
    )
    projected = projected + qkv_bias[:, None, None, :]
    queries = (rotate(split_heads(projected[0]), cosine, sine) * q_scale).astype(jnp.bfloat16)
    keys = rotate(split_heads(projected[1]), cosine, sine).astype(jnp.bfloat16)
    values_low = split_heads(projected[2]).astype(jnp.bfloat16)
    mixed_heads, log_total = lax.map(attend, (queries, keys, values_low, segments))
    mixed = join_heads(mixed_heads).astype(jnp.bfloat16)
    attn_part = lax.psum_scatter(
        jnp.dot(
            device_rows(mixed, lax.axis_size("tensor") * (groups * local_rows)),
            out_weight,
            preferred_element_type=jnp.float32,
        ),
        "tensor",
        scatter_dimension=0,
        tiled=True,
    )
    attn_part = attn_part.reshape(groups, local_rows, model_width)
    first_sum = tokens.astype(jnp.float32) + (attn_part + out_bias)
    normed, scaled_one, inv_one = norm_forward(first_sum, gain_one, shift_one)
    whole_normed = lax.all_gather(normed.astype(jnp.bfloat16), "tensor", axis=1, tiled=True)
    hidden = (
        jnp.einsum("gld,df->glf", whole_normed, up_weight, preferred_element_type=jnp.float32)
        + up_bias
    )
    active = jax.nn.gelu(hidden, approximate=False).astype(jnp.bfloat16)
    ffn_part = lax.psum_scatter(
        jnp.dot(
            device_rows(active, lax.axis_size("tensor") * (groups * local_rows)),
            down_weight,
            preferred_element_type=jnp.float32,
        ),
        "tensor",
        scatter_dimension=0,
        tiled=True,
    )
    second_sum = normed + (ffn_part.reshape(groups, local_rows, model_width) + down_bias)
    result, scaled_two, inv_two = norm_forward(second_sum, gain_two, shift_two)
    result_low = result.astype(jnp.bfloat16)
    embedded = jnp.einsum(
        "gld,dp->glp", result_low, proj_weight, preferred_element_type=jnp.float32
    )
    grad_result = out_grad.astype(jnp.float32) + jnp.einsum(
        "glp,dp->gld", embed_grad, proj_weight, preferred_element_type=jnp.float32
    )
    proj_grad = jnp.einsum(
        "gld,glp->dp", result_low, embed_grad, preferred_element_type=jnp.float32
    )
    grad_second, gain_two_grad, shift_two_grad = norm_backward(
        grad_result, scaled_two, inv_two, gain_two
    )
    second_low = grad_second.astype(jnp.bfloat16)
    down_bias_grad = jnp.sum(second_low.astype(jnp.float32), axis=(0, 1))
    whole_second = lax.all_gather(second_low, "tensor", axis=1, tiled=True)
    down_weight_grad = jnp.einsum(
        "glf,gld->fd", active, whole_second, preferred_element_type=jnp.float32
    )
    grad_active = jnp.einsum(
        "gld,fd->glf", whole_second, down_weight, preferred_element_type=jnp.float32
    )
    gelu_pull = jax.vjp(lambda field: jax.nn.gelu(field, approximate=False), hidden)[1]
    grad_hidden = gelu_pull(grad_active)[0].astype(jnp.bfloat16)
    up_bias_grad = jnp.sum(grad_hidden.astype(jnp.float32), axis=(0, 1))
    up_weight_grad = jnp.einsum(
        "gld,glf->df", whole_normed, grad_hidden, preferred_element_type=jnp.float32
    )
    ffn_back = lax.psum_scatter(
        jnp.einsum(
            "nf,df->nd",
            device_rows(grad_hidden, lax.axis_size("tensor") * (groups * local_rows)),
            up_weight,
            preferred_element_type=jnp.float32,
        ),
        "tensor",
        scatter_dimension=0,
        tiled=True,
    )
    grad_normed = grad_second + ffn_back.reshape(groups, local_rows, model_width)
    grad_first, gain_one_grad, shift_one_grad = norm_backward(
        grad_normed, scaled_one, inv_one, gain_one
    )
    first_low = grad_first.astype(jnp.bfloat16)
    out_bias_grad = jnp.sum(first_low.astype(jnp.float32), axis=(0, 1))
    whole_first = lax.all_gather(first_low, "tensor", axis=1, tiled=True)
    out_weight_grad = jnp.einsum(
        "glh,gld->hd", mixed, whole_first, preferred_element_type=jnp.float32
    )
    grad_mixed = jnp.einsum(
        "gld,hd->glh", whole_first, out_weight, preferred_element_type=jnp.float32
    )
    grad_mixed = split_heads(grad_mixed.astype(jnp.bfloat16))
    grad_queries, grad_keys, grad_values = lax.map(
        attend_back, (queries, keys, values_low, segments, log_total, grad_mixed)
    )
    grad_queries = rotate_back(grad_queries * q_scale, cosine, sine)
    grad_keys = rotate_back(grad_keys, cosine, sine)
    grad_qkv = jnp.stack(
        [join_heads(grad_queries), join_heads(grad_keys), join_heads(grad_values)]
    ).astype(jnp.bfloat16)
    qkv_bias_grad = jnp.sum(grad_qkv.astype(jnp.float32), axis=(1, 2))
    qkv_weight_grad = jnp.einsum(
        "gld,cgle->cde", whole_tokens, grad_qkv, preferred_element_type=jnp.float32
    )
    joined_grad = grad_qkv.transpose(1, 2, 0, 3).reshape(groups, length, 3 * heads_here * HEAD_DIM)
    joined_weight = qkv_weight.transpose(1, 0, 2).reshape(model_width, 3 * heads_here * HEAD_DIM)
    input_back = lax.psum_scatter(
        jnp.einsum(
            "ne,de->nd",
            device_rows(joined_grad, groups * local_rows * lax.axis_size("tensor")),
            joined_weight,
            preferred_element_type=jnp.float32,
        ).astype(jnp.bfloat16),
        "tensor",
        scatter_dimension=0,
        tiled=True,
    ).astype(jnp.float32)
    tokens_grad = grad_first + input_back.reshape(groups, local_rows, model_width)
    sharded_grads = (
        qkv_weight_grad,
        qkv_bias_grad,
        out_weight_grad,
        up_weight_grad,
        up_bias_grad,
        down_weight_grad,
    )
    shared_grads = (
        out_bias_grad,
        gain_one_grad,
        shift_one_grad,
        down_bias_grad,
        gain_two_grad,
        shift_two_grad,
        proj_grad,
    )
    return (result_low, embedded.astype(jnp.bfloat16), tokens_grad, sharded_grads, shared_grads)


def per_device(
    tokens,
    segments,
    qkv_weight,
    qkv_bias,
    out_weight,
    out_bias,
    gain_one,
    shift_one,
    up_weight,
    up_bias,
    down_weight,
    down_bias,
    gain_two,
    shift_two,
    proj_weight,
    out_grad,
    embed_grad,
):
    weights = (
        qkv_weight,
        qkv_bias,
        out_weight,
        out_bias,
        gain_one,
        shift_one,
        up_weight,
        up_bias,
        down_weight,
        down_bias,
        gain_two,
        shift_two,
        proj_weight,
    )

    def one_seq(running, per_seq):
        tok_row, seg_row, dy_row, de_row = per_seq
        results = process(tok_row[None], seg_row[None], dy_row[None], de_row[None], weights)
        running = jax.tree.map(jnp.add, running, (results[3], results[4]))
        return (running, (results[0][0], results[1][0], results[2][0]))

    empty_grads = (
        tuple(
            (
                jnp.zeros(w.shape, jnp.float32)
                for w in (qkv_weight, qkv_bias, out_weight, up_weight, up_bias, down_weight)
            )
        ),
        tuple(
            (
                jnp.zeros(w.shape, jnp.float32)
                for w in (
                    out_bias,
                    gain_one,
                    shift_one,
                    down_bias,
                    gain_two,
                    shift_two,
                    proj_weight,
                )
            )
        ),
    )
    (sharded_grads, shared_grads), (layer_out, embeddings, tokens_grad) = lax.scan(
        one_seq, empty_grads, (tokens, segments, out_grad, embed_grad)
    )
    sharded_grads = jax.tree.map(
        lambda part: part.astype(jnp.float32), lax.psum(as_sent(sharded_grads), "dp")
    )
    shared_grads = lax.psum(shared_grads, ("dp", "tensor"))
    return (
        layer_out,
        embeddings,
        tokens_grad,
        sharded_grads[0],
        sharded_grads[1],
        sharded_grads[2],
        shared_grads[0],
        shared_grads[1],
        shared_grads[2],
        sharded_grads[3],
        sharded_grads[4],
        sharded_grads[5],
        shared_grads[3],
        shared_grads[4],
        shared_grads[5],
        shared_grads[6],
    )


def solution(mesh):
    in_specs = (
        P("dp", "tensor", None),
        P("dp", None),
        P(None, None, "tensor"),
        P(None, "tensor"),
        P("tensor", None),
        P(),
        P(),
        P(),
        P(None, "tensor"),
        P("tensor"),
        P("tensor", None),
        P(),
        P(),
        P(),
        P(),
        P("dp", "tensor", None),
        P("dp", "tensor", None),
    )
    out_specs = (
        P("dp", "tensor", None),
        P("dp", "tensor", None),
        P("dp", "tensor", None),
        P(None, None, "tensor"),
        P(None, "tensor"),
        P("tensor", None),
        P(),
        P(),
        P(),
        P(None, "tensor"),
        P("tensor"),
        P("tensor", None),
        P(),
        P(),
        P(),
        P(),
    )
    return jax.shard_map(
        per_device, mesh=mesh, in_specs=in_specs, out_specs=out_specs, check_vma=False
    )
```

profile of v0, /device:TPU:0, one launch (start us, length us, event | category | flops | bytes accessed | tf_op | source)
XLA Modules:
  0.0 1448.8 jit_solution(7580111649799563815)
XLA Ops:
  10.8 1174.9 %while.6 = (s32[]{:T(128)}, f32[3,1024,256]{1,2,0:T(8,128)}, f32[3,256]{1,0:T(4,128)}, f32[256,1024]{1,0:T(8,128)}, f32[1024,1024]{1,0:T(8,128)}, /*index=5*/f32...) while((s32[]{:T(128)}, f32[3,1024,256]{1,2,0:T(8,128)}, ...), condition=%wide.region_26.27_spmd.clone, body=%wide.region_0.26_spmd.clone.sunk | while | flops 23216961536 | bytes 635246848 | solution.py:351
  17.6 44.3 %all-gather.5.cloned.1.call-done = bf16[1,1024,1024]{2,1,0:T(8,128)(2,1)} async-done(((bf16[1,256,1024]{2,1,0:T(8,128)(2,1)}), bf16[1,1024,1024]{2,1,0:T(8,128)(2,1)}) %all-gather.5.cloned.1.call-update) | async-done | bytes 2097168 | tf_op jit(solution)/shard_map/while/body/eval_jaxpr/all_gather | solution.py:148
  74.1 8.8 fusion.227
  95.1 75.3 %reduce-scatter.5.cloned.1.call-done = f32[256,1024]{1,0:T(8,128)} async-done(((f32[1024,1024]{1,0:T(8,128)}), f32[256,1024]{1,0:T(8,128)}) %reduce-scatter.5.cloned.1.call-update) | async-done | bytes 1048592 | tf_op jit(solution)/shard_map/while/body/eval_jaxpr/reduce_scatter | solution.py:158
  173.2 46.6 %all-gather.7.cloned.1.call-done = bf16[1,1024,1024]{2,1,0:T(8,128)(2,1)} async-done(((bf16[1,256,1024]{2,1,0:T(8,128)(2,1)}), bf16[1,1024,1024]{2,1,0:T(8,128)(2,1)}) %all-gather.7.cloned.1.call-update) | async-done | bytes 2097168 | tf_op jit(solution)/shard_map/while/body/eval_jaxpr/all_gather | solution.py:171
  219.8 14.8 %multiply_convert_fusion.4 = (bf16[1024,1024]{1,0:T(8,128)(2,1)S(1)}, f32[1024,1024]{1,0:T(8,128)}, f32[1024,1024]{1,0:T(8,128)}) fusion(f32[1024]{0:T(1024)S(1)} %copy-done.58, bf16[1024,1024]{1,0:T(8,128)(2,1)} %get-tuple-element.999, bf16[1,1024,1024]{2,1,0:T(8,128)(2,1)} %all-gather.7.cloned.1.call-done), kind=kOutput, calls=%fused_computation.17.clone.1 | convolution fusion | flops 2216689664 | bytes 14684160 | tf_op jit(solution)/shard_map/while/body/eval_jaxpr/gld,df->glf/dot_general | solution.py:173
  240.3 75.6 %reduce-scatter.7.cloned.1.call-done = f32[256,1024]{1,0:T(8,128)} async-done(((f32[1024,1024]{1,0:T(8,128)}), f32[256,1024]{1,0:T(8,128)}) %reduce-scatter.7.cloned.1.call-update) | async-done | bytes 1048592 | tf_op jit(solution)/shard_map/while/body/eval_jaxpr/reduce_scatter | solution.py:177
  322.1 46.0 %all-gather.9.cloned.1.call-done = bf16[1,1024,1024]{2,1,0:T(8,128)(2,1)} async-done(((bf16[1,256,1024]{2,1,0:T(8,128)(2,1)}), bf16[1,1024,1024]{2,1,0:T(8,128)(2,1)}) %all-gather.9.cloned.1.call-update) | async-done | bytes 2097168 | tf_op jit(solution)/shard_map/while/body/eval_jaxpr/all_gather | solution.py:204
  368.0 8.5 convert_reduce_fusion.9
  382.3 75.6 %reduce-scatter.9.cloned.1.call-done = f32[256,1024]{1,0:T(8,128)} async-done(((f32[1024,1024]{1,0:T(8,128)}), f32[256,1024]{1,0:T(8,128)}) %reduce-scatter.9.cloned.1.call-update) | async-done | bytes 1048592 | tf_op jit(solution)/shard_map/while/body/eval_jaxpr/reduce_scatter | solution.py:217
  461.7 46.5 %all-gather.11.cloned.1.call-done = bf16[1,1024,1024]{2,1,0:T(8,128)(2,1)} async-done(((bf16[1,256,1024]{2,1,0:T(8,128)(2,1)}), bf16[1,1024,1024]{2,1,0:T(8,128)(2,1)}) %all-gather.11.cloned.1.call-update) | async-done | bytes 2097168 | tf_op jit(solution)/shard_map/while/body/eval_jaxpr/all_gather | solution.py:234
  510.6 8.7 fusion.236
  519.4 11.8 multiply_reduce_fusion.18
  531.2 12.2 multiply_convert_fusion.5
  576.4 19.7 %reduce-scatter.11.cloned.1.call-done = bf16[256,1024]{1,0:T(8,128)(2,1)} async-done(((bf16[1024,1024]{1,0:T(8,128)(2,1)}), bf16[256,1024]{1,0:T(8,128)(2,1)}) %reduce-scatter.11.cloned.1.call-update) | async-done | bytes 524304 | tf_op jit(solution)/shard_map/while/body/eval_jaxpr/reduce_scatter | solution.py:256
  605.3 40.9 %all-gather.5.cloned.1.call-done = bf16[1,1024,1024]{2,1,0:T(8,128)(2,1)} async-done(((bf16[1,256,1024]{2,1,0:T(8,128)(2,1)}), bf16[1,1024,1024]{2,1,0:T(8,128)(2,1)}) %all-gather.5.cloned.1.call-update) | async-done | bytes 2097168 | tf_op jit(solution)/shard_map/while/body/eval_jaxpr/all_gather | solution.py:148
  658.5 8.8 fusion.227
  679.5 75.1 %reduce-scatter.5.cloned.1.call-done = f32[256,1024]{1,0:T(8,128)} async-done(((f32[1024,1024]{1,0:T(8,128)}), f32[256,1024]{1,0:T(8,128)}) %reduce-scatter.5.cloned.1.call-update) | async-done | bytes 1048592 | tf_op jit(solution)/shard_map/while/body/eval_jaxpr/reduce_scatter | solution.py:158
  757.5 46.6 %all-gather.7.cloned.1.call-done = bf16[1,1024,1024]{2,1,0:T(8,128)(2,1)} async-done(((bf16[1,256,1024]{2,1,0:T(8,128)(2,1)}), bf16[1,1024,1024]{2,1,0:T(8,128)(2,1)}) %all-gather.7.cloned.1.call-update) | async-done | bytes 2097168 | tf_op jit(solution)/shard_map/while/body/eval_jaxpr/all_gather | solution.py:171
  804.1 14.8 %multiply_convert_fusion.4 = (bf16[1024,1024]{1,0:T(8,128)(2,1)S(1)}, f32[1024,1024]{1,0:T(8,128)}, f32[1024,1024]{1,0:T(8,128)}) fusion(f32[1024]{0:T(1024)S(1)} %copy-done.58, bf16[1024,1024]{1,0:T(8,128)(2,1)} %get-tuple-element.999, bf16[1,1024,1024]{2,1,0:T(8,128)(2,1)} %all-gather.7.cloned.1.call-done), kind=kOutput, calls=%fused_computation.17.clone.1 | convolution fusion | flops 2216689664 | bytes 14684160 | tf_op jit(solution)/shard_map/while/body/eval_jaxpr/gld,df->glf/dot_general | solution.py:173
  824.6 75.6 %reduce-scatter.7.cloned.1.call-done = f32[256,1024]{1,0:T(8,128)} async-done(((f32[1024,1024]{1,0:T(8,128)}), f32[256,1024]{1,0:T(8,128)}) %reduce-scatter.7.cloned.1.call-update) | async-done | bytes 1048592 | tf_op jit(solution)/shard_map/while/body/eval_jaxpr/reduce_scatter | solution.py:177
  906.0 46.4 %all-gather.9.cloned.1.call-done = bf16[1,1024,1024]{2,1,0:T(8,128)(2,1)} async-done(((bf16[1,256,1024]{2,1,0:T(8,128)(2,1)}), bf16[1,1024,1024]{2,1,0:T(8,128)(2,1)}) %all-gather.9.cloned.1.call-update) | async-done | bytes 2097168 | tf_op jit(solution)/shard_map/while/body/eval_jaxpr/all_gather | solution.py:204
  966.6 75.6 %reduce-scatter.9.cloned.1.call-done = f32[256,1024]{1,0:T(8,128)} async-done(((f32[1024,1024]{1,0:T(8,128)}), f32[256,1024]{1,0:T(8,128)}) %reduce-scatter.9.cloned.1.call-update) | async-done | bytes 1048592 | tf_op jit(solution)/shard_map/while/body/eval_jaxpr/reduce_scatter | solution.py:217
  1046.0 46.5 %all-gather.11.cloned.1.call-done = bf16[1,1024,1024]{2,1,0:T(8,128)(2,1)} async-done(((bf16[1,256,1024]{2,1,0:T(8,128)(2,1)}), bf16[1,1024,1024]{2,1,0:T(8,128)(2,1)}) %all-gather.11.cloned.1.call-update) | async-done | bytes 2097168 | tf_op jit(solution)/shard_map/while/body/eval_jaxpr/all_gather | solution.py:234
  1095.0 8.7 fusion.236
  1103.7 11.8 multiply_reduce_fusion.18
  1115.5 12.3 multiply_convert_fusion.5
  1163.0 17.5 %reduce-scatter.11.cloned.1.call-done = bf16[256,1024]{1,0:T(8,128)(2,1)} async-done(((bf16[1024,1024]{1,0:T(8,128)(2,1)}), bf16[256,1024]{1,0:T(8,128)(2,1)}) %reduce-scatter.11.cloned.1.call-update) | async-done | bytes 524304 | tf_op jit(solution)/shard_map/while/body/eval_jaxpr/reduce_scatter | solution.py:256
  1197.3 13.8 all-reduce.1
  1212.2 40.5 %all-reduce = (f32[1024]{0:T(1024)}, f32[1024]{0:T(1024)}, f32[1024]{0:T(1024)}, f32[1024]{0:T(1024)}, f32[1024]{0:T(1024)}, /*index=5*/f32[1024]{0:T(1024)}) all-reduce(f32[1024]{0:T(1024)S(1)} %copy-done.49, f32[1024]{0:T(1024)S(1)} %copy-done.46, f32[1024]{0:T(1024)S(1)} %copy-done.43, ...), channel_id=1, replica_groups=mesh['dp'=8,'tensor'=4] {'dp','tensor'}, use_global_device_ids=true, to_apply=%region_30.31 | all-reduce | flops 6144 | bytes 49152 | tf_op jit(solution)/shard_map/psum | solution.py:357
  1252.7 48.6 %all-reduce.8.cloned.1.call-done = (bf16[3,1024,256]{2,1,0:T(8,128)(2,1)}, bf16[256,1024]{1,0:T(8,128)(2,1)}, bf16[1024,1024]{1,0:T(8,128)(2,1)}, bf16[1024,1024]{1,0:T(8,128)(2,1)}) async-done(((bf16[3,1024,256]{2,1,0:T(8,128)(2,1)}, bf16[256,1024]{1,0:T(8,128)(2,1)}, bf16[1024,1024]{1,0:T(8,128)(2,1)}, bf16[1024,1024]{1,0:T(8,128)(2,1)}), (bf16[3,1024,256]{2,1,0:T(8,128)(2,1)}, ...) | async-done | bytes 6291472 | tf_op jit(solution)/shard_map/psum | solution.py:355
  1311.9 127.1 %all-reduce.6.cloned.1.call-done = f32[1024,288]{0,1:T(8,128)} async-done(((f32[1024,288]{0,1:T(8,128)}), f32[1024,288]{0,1:T(8,128)}) %all-reduce.6.cloned.1.call-update) | async-done | bytes 1179664 | tf_op jit(solution)/shard_map/psum | solution.py:357
  (429 shorter events, 223.2 us)
Async XLA Ops:
  10.8 51.1 %all-gather.5.cloned.1.call-start = ((), (), s32[]{:S(2)}) async-start(), calls=%async_computation.6 | async-start | bytes 2621440 | tf_op jit(solution)/shard_map/while/body/eval_jaxpr/all_gather | solution.py:148
  12.7 157.6 %reduce-scatter.5.cloned.1.call-start = ((), (), s32[]{:S(2)}) async-start(), calls=%async_computation.7 | async-start | bytes 5242880 | tf_op jit(solution)/shard_map/while/body/eval_jaxpr/reduce_scatter | solution.py:158
  94.6 75.7 %copy-start.17 = (bf16[2,256,1024]{2,1,0:T(8,128)(2,1)S(1)}, bf16[2,256,1024]{2,1,0:T(8,128)(2,1)}, u32[]{:S(2)}) copy-start(bf16[2,256,1024]{2,1,0:T(8,128)(2,1)} %get-tuple-element.992) | copy-start | bytes 3145732 | tf_op jit(solution)/shard_map/while
  94.6 75.7 %copy-start.50 = (f32[1024]{0:T(1024)S(1)}, f32[1024]{0:T(1024)}, u32[]{:S(2)}) copy-start(f32[1024]{0:T(1024)} %get-tuple-element.996) | copy-start | bytes 12292 | tf_op jit(solution)/shard_map/while
  94.6 77.4 %copy-start.28 = (f32[1024]{0:T(1024)S(1)}, f32[1024]{0:T(1024)}, u32[]{:S(2)}) copy-start(f32[1024]{0:T(1024)} %get-tuple-element.997) | copy-start | bytes 12292 | tf_op jit(solution)/shard_map/while
  94.6 77.4 %copy-start.30 = (f32[1024]{0:T(1024)S(1)}, f32[1024]{0:T(1024)}, u32[]{:S(2)}) copy-start(f32[1024]{0:T(1024)} %get-tuple-element.998) | copy-start | bytes 12292 | tf_op jit(solution)/shard_map/while
  94.6 125.1 %copy-start.58 = (f32[1024]{0:T(1024)S(1)}, f32[1024]{0:T(1024)}, u32[]{:S(2)}) copy-start(f32[1024]{0:T(1024)} %get-tuple-element.1000) | copy-start | bytes 12292 | tf_op jit(solution)/shard_map/while
  94.7 125.1 %all-gather.7.cloned.1.call-start = ((), (), s32[]{:S(2)}) async-start(), calls=%async_computation.8 | async-start | bytes 2621440 | tf_op jit(solution)/shard_map/while/body/eval_jaxpr/all_gather | solution.py:171
  173.1 142.7 %reduce-scatter.7.cloned.1.call-start = ((), (), s32[]{:S(2)}) async-start(), calls=%async_computation.9 | async-start | bytes 5242880 | tf_op jit(solution)/shard_map/while/body/eval_jaxpr/reduce_scatter | solution.py:177
  240.2 75.7 %copy-start.51 = (f32[1024]{0:T(1024)S(1)}, f32[1024]{0:T(1024)}, u32[]{:S(2)}) copy-start(f32[1024]{0:T(1024)} %get-tuple-element.1002) | copy-start | bytes 12292 | tf_op jit(solution)/shard_map/while
  240.2 77.6 %copy-start.31 = (f32[1024]{0:T(1024)S(1)}, f32[1024]{0:T(1024)}, u32[]{:S(2)}) copy-start(f32[1024]{0:T(1024)} %get-tuple-element.1006) | copy-start | bytes 12292 | tf_op jit(solution)/shard_map/while
  240.3 127.8 %all-gather.9.cloned.1.call-start = ((), (), s32[]{:S(2)}) async-start(), calls=%async_computation.10 | async-start | bytes 2621440 | tf_op jit(solution)/shard_map/while/body/eval_jaxpr/all_gather | solution.py:204
  321.4 136.4 %reduce-scatter.9.cloned.1.call-start = ((), (), s32[]{:S(2)}) async-start(), calls=%async_computation.11 | async-start | bytes 5242880 | tf_op jit(solution)/shard_map/while/body/eval_jaxpr/reduce_scatter | solution.py:217
  382.2 125.9 %all-gather.11.cloned.1.call-start = ((), (), s32[]{:S(2)}) async-start(), calls=%async_computation.12 | async-start | bytes 2621440 | tf_op jit(solution)/shard_map/while/body/eval_jaxpr/all_gather | solution.py:234
  461.6 134.5 %reduce-scatter.11.cloned.1.call-start = ((), (), s32[]{:S(2)}) async-start(), calls=%async_computation.13 | async-start | bytes 2621440 | tf_op jit(solution)/shard_map/while/body/eval_jaxpr/reduce_scatter | solution.py:256
  598.5 47.7 %all-gather.5.cloned.1.call-start = ((), (), s32[]{:S(2)}) async-start(), calls=%async_computation.6 | async-start | bytes 2621440 | tf_op jit(solution)/shard_map/while/body/eval_jaxpr/all_gather | solution.py:148
  600.5 154.2 %reduce-scatter.5.cloned.1.call-start = ((), (), s32[]{:S(2)}) async-start(), calls=%async_computation.7 | async-start | bytes 5242880 | tf_op jit(solution)/shard_map/while/body/eval_jaxpr/reduce_scatter | solution.py:158
  679.0 75.7 %copy-start.17 = (bf16[2,256,1024]{2,1,0:T(8,128)(2,1)S(1)}, bf16[2,256,1024]{2,1,0:T(8,128)(2,1)}, u32[]{:S(2)}) copy-start(bf16[2,256,1024]{2,1,0:T(8,128)(2,1)} %get-tuple-element.992) | copy-start | bytes 3145732 | tf_op jit(solution)/shard_map/while
  679.0 75.7 %copy-start.50 = (f32[1024]{0:T(1024)S(1)}, f32[1024]{0:T(1024)}, u32[]{:S(2)}) copy-start(f32[1024]{0:T(1024)} %get-tuple-element.996) | copy-start | bytes 12292 | tf_op jit(solution)/shard_map/while
  679.0 77.4 %copy-start.28 = (f32[1024]{0:T(1024)S(1)}, f32[1024]{0:T(1024)}, u32[]{:S(2)}) copy-start(f32[1024]{0:T(1024)} %get-tuple-element.997) | copy-start | bytes 12292 | tf_op jit(solution)/shard_map/while
  679.0 77.4 %copy-start.30 = (f32[1024]{0:T(1024)S(1)}, f32[1024]{0:T(1024)}, u32[]{:S(2)}) copy-start(f32[1024]{0:T(1024)} %get-tuple-element.998) | copy-start | bytes 12292 | tf_op jit(solution)/shard_map/while
  679.0 125.1 %copy-start.58 = (f32[1024]{0:T(1024)S(1)}, f32[1024]{0:T(1024)}, u32[]{:S(2)}) copy-start(f32[1024]{0:T(1024)} %get-tuple-element.1000) | copy-start | bytes 12292 | tf_op jit(solution)/shard_map/while
  679.0 125.1 %all-gather.7.cloned.1.call-start = ((), (), s32[]{:S(2)}) async-start(), calls=%async_computation.8 | async-start | bytes 2621440 | tf_op jit(solution)/shard_map/while/body/eval_jaxpr/all_gather | solution.py:171
  757.5 142.7 %reduce-scatter.7.cloned.1.call-start = ((), (), s32[]{:S(2)}) async-start(), calls=%async_computation.9 | async-start | bytes 5242880 | tf_op jit(solution)/shard_map/while/body/eval_jaxpr/reduce_scatter | solution.py:177
  824.6 75.7 %copy-start.51 = (f32[1024]{0:T(1024)S(1)}, f32[1024]{0:T(1024)}, u32[]{:S(2)}) copy-start(f32[1024]{0:T(1024)} %get-tuple-element.1002) | copy-start | bytes 12292 | tf_op jit(solution)/shard_map/while
  824.6 77.6 %copy-start.31 = (f32[1024]{0:T(1024)S(1)}, f32[1024]{0:T(1024)}, u32[]{:S(2)}) copy-start(f32[1024]{0:T(1024)} %get-tuple-element.1006) | copy-start | bytes 12292 | tf_op jit(solution)/shard_map/while
  824.6 127.8 %all-gather.9.cloned.1.call-start = ((), (), s32[]{:S(2)}) async-start(), calls=%async_computation.10 | async-start | bytes 2621440 | tf_op jit(solution)/shard_map/while/body/eval_jaxpr/all_gather | solution.py:204
  905.8 136.4 %reduce-scatter.9.cloned.1.call-start = ((), (), s32[]{:S(2)}) async-start(), calls=%async_computation.11 | async-start | bytes 5242880 | tf_op jit(solution)/shard_map/while/body/eval_jaxpr/reduce_scatter | solution.py:217
  966.6 125.9 %all-gather.11.cloned.1.call-start = ((), (), s32[]{:S(2)}) async-start(), calls=%async_computation.12 | async-start | bytes 2621440 | tf_op jit(solution)/shard_map/while/body/eval_jaxpr/all_gather | solution.py:234
  1045.9 134.6 %reduce-scatter.11.cloned.1.call-start = ((), (), s32[]{:S(2)}) async-start(), calls=%async_computation.13 | async-start | bytes 2621440 | tf_op jit(solution)/shard_map/while/body/eval_jaxpr/reduce_scatter | solution.py:256
  1185.7 115.6 %all-reduce.8.cloned.1.call-start = ((), (), s32[]{:S(2)}) async-start(), calls=%async_computation.5 | async-start | bytes 12582912 | tf_op jit(solution)/shard_map/psum | solution.py:355
  1196.6 242.5 %all-reduce.6.cloned.1.call-start = ((), (), s32[]{:S(2)}) async-start(), calls=%async_computation.4 | async-start | bytes 2359296 | tf_op jit(solution)/shard_map/psum | solution.py:357
  (101 other events, 699.8 us)
Sparse Core Ops, SparseCore 0:
  13.2 48.6 all-gather.4
  94.8 75.4 reduce-scatter.4
  173.3 46.4 all-gather.6
  240.4 75.4 reduce-scatter.6
  321.6 46.4 all-gather.8
  382.4 75.4 reduce-scatter.8
  461.7 46.4 all-gather.10
  553.5 42.5 reduce-scatter.10
  600.9 45.2 all-gather.4
  679.1 75.4 reduce-scatter.4
  757.6 46.4 all-gather.6
  824.7 75.4 reduce-scatter.6
  905.9 46.4 all-gather.8
  966.7 75.4 reduce-scatter.8
  1046.0 46.4 all-gather.10
  1137.9 42.5 reduce-scatter.10
Sparse Core Ops, SparseCore 1:
  1196.7 104.6 all-reduce.7
  1308.1 130.9 all-reduce.5
where the time goes:
time: 1450 us
  waiting for transfers between devices  1030 us (71%)
  matrix products  209 us (14%)
  other arithmetic  99.4 us (7%)
  blocking collectives  54.2 us (4%)
  local copies, waits for them, and re-layouts  33.1 us (2%)
  between operations  15.6 us (1%)
    reduce_scatter x2, waiting for transfers between devices, process(): lax.psum_scatter(jnp.einsum('nf,df->nd', device_rows(grad_hidden, lax.axi...  151 us
    reduce_scatter x2, waiting for transfers between devices, process(): lax.psum_scatter(jnp.dot(device_rows(active, lax.axis_size('tensor') * (g...  151 us
    reduce_scatter x2, waiting for transfers between devices, process(): lax.psum_scatter(jnp.dot(device_rows(mixed, lax.axis_size('tensor') * (gr...  150 us
    psum x1, waiting for transfers between devices, per_device(): shared_grads = lax.psum(shared_grads, ('dp', 'tensor'))  127 us
    all_gather x2, waiting for transfers between devices, process(): lax.all_gather(normed.astype(jnp.bfloat16), 'tensor', axis=1, tiled=True)  93.1 us
    all_gather x2, waiting for transfers between devices, process(): whole_first = lax.all_gather(first_low, 'tensor', axis=1, tiled=True)  93 us
    all_gather x2, waiting for transfers between devices, process(): whole_second = lax.all_gather(second_low, 'tensor', axis=1, tiled=True)  92.3 us
    all_gather x2, waiting for transfers between devices, process(): whole_tokens = lax.all_gather(tokens, 'tensor', axis=1, tiled=True)  85.2 us
  transfers between devices with their start and end apart: 18, of which 18 were waited for; matrix products, arithmetic and copies ran while one was open for 4% of the time, Pallas kernels for 0%

commit v1 on v0

--- a/solution.py
+++ b/solution.py
@@ -6,6 +6,19 @@
 
 HEAD_DIM = 64
 eps = 1e-05
+
+
+def collect(value, axis, dim):
+    ways = lax.axis_size(axis)
+    up = [(d, (d + 1) % ways) for d in range(ways)]
+    down = [(d, (d - 1) % ways) for d in range(ways)]
+    earlier, later = ([value], [value])
+    for _ in range(ways // 2):
+        earlier.append(lax.ppermute(earlier[-1], axis, up))
+    for _ in range((ways - 1) // 2):
+        later.append(lax.ppermute(later[-1], axis, down))
+    line = jnp.concatenate([*earlier[::-1], *later[1:]], axis=dim)
+    return jnp.roll(line, (lax.axis_index(axis) - ways // 2) * value.shape[dim], axis=dim)
 
 
 def as_sent(array):
@@ -231,7 +244,7 @@
     )
     first_low = grad_first.astype(jnp.bfloat16)
     out_bias_grad = jnp.sum(first_low.astype(jnp.float32), axis=(0, 1))
-    whole_first = lax.all_gather(first_low, "tensor", axis=1, tiled=True)
+    whole_first = collect(first_low, "tensor", 1)
     out_weight_grad = jnp.einsum(
         "glh,gld->hd", mixed, whole_first, preferred_element_type=jnp.float32
     )

time: 1450 us -> 1450 us (level)
  waiting for transfers between devices: 1030 us -> 1010 us
    all_gather x2 -> x0, waiting for transfers between devices: 93 us -> none  [process(): whole_first = lax.all_gather(first_low, 'tensor', axis=1, tiled=True)]
    ppermute x0 -> x6, waiting for transfers between devices: none -> 64.5 us  [the longest x4 53.8 us: collect(): earlier.append(lax.ppermute(earlier[-1], axis, up))]
    while x212 -> x254, local copies, waits for them, and re-layouts: 18.8 us -> 30.1 us
  transfers between devices with their start and end apart: 18 -> 22, of which waited for: 18 -> 22; matrix products, arithmetic and copies ran while one was open for 4% -> 4% of each run, Pallas kernels for 0% -> 0%
where the time goes in v1:
time: 1450 us; the launch traced here: 1440 us
  waiting for transfers between devices  1010 us (70%)
  matrix products  205 us (14%)
  other arithmetic  99.1 us (7%)
  blocking collectives  54.2 us (4%)
  local copies, waits for them, and re-layouts  44.5 us (3%)
  between operations  15.6 us (1%)
    reduce_scatter x2, waiting for transfers between devices, process(): lax.psum_scatter(jnp.einsum('nf,df->nd', device_rows(grad_hidden, lax.axi...  151 us
    reduce_scatter x2, waiting for transfers between devices, process(): lax.psum_scatter(jnp.dot(device_rows(active, lax.axis_size('tensor') * (g...  151 us
    reduce_scatter x2, waiting for transfers between devices, process(): lax.psum_scatter(jnp.dot(device_rows(mixed, lax.axis_size('tensor') * (gr...  150 us
    psum x1, waiting for transfers between devices, per_device(): shared_grads = lax.psum(shared_grads, ('dp', 'tensor'))  127 us
    all_gather x2, waiting for transfers between devices, process(): lax.all_gather(normed.astype(jnp.bfloat16), 'tensor', axis=1, tiled=True)  93.1 us
    all_gather x2, waiting for transfers between devices, process(): whole_second = lax.all_gather(second_low, 'tensor', axis=1, tiled=True)  92.5 us
    all_gather x2, waiting for transfers between devices, process(): whole_tokens = lax.all_gather(tokens, 'tensor', axis=1, tiled=True)  85.1 us
    ppermute x4, waiting for transfers between devices, collect(): earlier.append(lax.ppermute(earlier[-1], axis, up))  53.8 us
  transfers between devices with their start and end apart: 22, of which 22 were waited for; matrix products, arithmetic and copies ran while one was open for 4% of the time, Pallas kernels for 0%

profile of v1, /device:TPU:0, one launch (start us, length us, event | category | flops | bytes accessed | tf_op | source)
XLA Modules:
  0.0 1442.6 jit_solution(17659754128190948934)
XLA Ops:
  10.8 1168.6 %while.8 = (s32[]{:T(128)}, f32[3,1024,256]{1,2,0:T(8,128)}, f32[3,256]{1,0:T(4,128)}, f32[256,1024]{1,0:T(8,128)}, f32[1024,1024]{1,0:T(8,128)}, /*index=5*/f32...) while((s32[]{:T(128)}, f32[3,1024,256]{1,2,0:T(8,128)}, ...), condition=%wide.region_26.27_spmd.clone, body=%wide.region_0.26_spmd.clone.sunk | while | flops 23216961536 | bytes 667883968 | solution.py:364
  17.6 44.3 %all-gather.4.cloned.1.call-done = bf16[1,1024,1024]{2,1,0:T(8,128)(2,1)} async-done(((bf16[1,256,1024]{2,1,0:T(8,128)(2,1)}), bf16[1,1024,1024]{2,1,0:T(8,128)(2,1)}) %all-gather.4.cloned.1.call-update) | async-done | bytes 2097168 | tf_op jit(solution)/shard_map/while/body/eval_jaxpr/all_gather | solution.py:161
  74.1 8.8 fusion.231
  95.2 75.1 %reduce-scatter.5.cloned.1.call-done = f32[256,1024]{1,0:T(8,128)} async-done(((f32[1024,1024]{1,0:T(8,128)}), f32[256,1024]{1,0:T(8,128)}) %reduce-scatter.5.cloned.1.call-update) | async-done | bytes 1048592 | tf_op jit(solution)/shard_map/while/body/eval_jaxpr/reduce_scatter | solution.py:171
  173.2 46.5 %all-gather.6.cloned.1.call-done = bf16[1,1024,1024]{2,1,0:T(8,128)(2,1)} async-done(((bf16[1,256,1024]{2,1,0:T(8,128)(2,1)}), bf16[1,1024,1024]{2,1,0:T(8,128)(2,1)}) %all-gather.6.cloned.1.call-update) | async-done | bytes 2097168 | tf_op jit(solution)/shard_map/while/body/eval_jaxpr/all_gather | solution.py:184
  219.7 14.9 %multiply_convert_fusion.4 = (bf16[1024,1024]{1,0:T(8,128)(2,1)S(1)}, f32[1024,1024]{1,0:T(8,128)}, f32[1024,1024]{1,0:T(8,128)}) fusion(f32[1024]{0:T(1024)S(1)} %copy-done.65, bf16[1024,1024]{1,0:T(8,128)(2,1)} %get-tuple-element.1255, bf16[1,1024,1024]{2,1,0:T(8,128)(2,1)} %all-gather.6.cloned.1.call-done), kind=kOutput, calls=%fused_computation.17.clone.1 | convolution fusion | flops 2216689664 | bytes 14684160 | tf_op jit(solution)/shard_map/while/body/eval_jaxpr/gld,df->glf/dot_general | solution.py:186
  240.4 75.6 %reduce-scatter.7.cloned.1.call-done = f32[256,1024]{1,0:T(8,128)} async-done(((f32[1024,1024]{1,0:T(8,128)}), f32[256,1024]{1,0:T(8,128)}) %reduce-scatter.7.cloned.1.call-update) | async-done | bytes 1048592 | tf_op jit(solution)/shard_map/while/body/eval_jaxpr/reduce_scatter | solution.py:190
  321.8 46.4 %all-gather.8.cloned.1.call-done = bf16[1,1024,1024]{2,1,0:T(8,128)(2,1)} async-done(((bf16[1,256,1024]{2,1,0:T(8,128)(2,1)}), bf16[1,1024,1024]{2,1,0:T(8,128)(2,1)}) %all-gather.8.cloned.1.call-update) | async-done | bytes 2097168 | tf_op jit(solution)/shard_map/while/body/eval_jaxpr/all_gather | solution.py:217
  382.4 75.6 %reduce-scatter.9.cloned.1.call-done = f32[256,1024]{1,0:T(8,128)} async-done(((f32[1024,1024]{1,0:T(8,128)}), f32[256,1024]{1,0:T(8,128)}) %reduce-scatter.9.cloned.1.call-update) | async-done | bytes 1048592 | tf_op jit(solution)/shard_map/while/body/eval_jaxpr/reduce_scatter | solution.py:230
  463.7 14.0 collective-permute-done
  481.6 12.9 collective-permute-done.1
  514.1 11.8 multiply_reduce_fusion.18
  526.0 12.3 multiply_convert_fusion.5
  570.8 22.2 %reduce-scatter.11.cloned.1.call-done = bf16[256,1024]{1,0:T(8,128)(2,1)} async-done(((bf16[1024,1024]{1,0:T(8,128)(2,1)}), bf16[256,1024]{1,0:T(8,128)(2,1)}) %reduce-scatter.11.cloned.1.call-update) | async-done | bytes 524304 | tf_op jit(solution)/shard_map/while/body/eval_jaxpr/reduce_scatter | solution.py:269
  602.1 40.9 %all-gather.4.cloned.1.call-done = bf16[1,1024,1024]{2,1,0:T(8,128)(2,1)} async-done(((bf16[1,256,1024]{2,1,0:T(8,128)(2,1)}), bf16[1,1024,1024]{2,1,0:T(8,128)(2,1)}) %all-gather.4.cloned.1.call-update) | async-done | bytes 2097168 | tf_op jit(solution)/shard_map/while/body/eval_jaxpr/all_gather | solution.py:161
  655.2 8.8 fusion.231
  676.0 75.4 %reduce-scatter.5.cloned.1.call-done = f32[256,1024]{1,0:T(8,128)} async-done(((f32[1024,1024]{1,0:T(8,128)}), f32[256,1024]{1,0:T(8,128)}) %reduce-scatter.5.cloned.1.call-update) | async-done | bytes 1048592 | tf_op jit(solution)/shard_map/while/body/eval_jaxpr/reduce_scatter | solution.py:171
  754.3 46.6 %all-gather.6.cloned.1.call-done = bf16[1,1024,1024]{2,1,0:T(8,128)(2,1)} async-done(((bf16[1,256,1024]{2,1,0:T(8,128)(2,1)}), bf16[1,1024,1024]{2,1,0:T(8,128)(2,1)}) %all-gather.6.cloned.1.call-update) | async-done | bytes 2097168 | tf_op jit(solution)/shard_map/while/body/eval_jaxpr/all_gather | solution.py:184
  800.8 14.9 %multiply_convert_fusion.4 = (bf16[1024,1024]{1,0:T(8,128)(2,1)S(1)}, f32[1024,1024]{1,0:T(8,128)}, f32[1024,1024]{1,0:T(8,128)}) fusion(f32[1024]{0:T(1024)S(1)} %copy-done.65, bf16[1024,1024]{1,0:T(8,128)(2,1)} %get-tuple-element.1255, bf16[1,1024,1024]{2,1,0:T(8,128)(2,1)} %all-gather.6.cloned.1.call-done), kind=kOutput, calls=%fused_computation.17.clone.1 | convolution fusion | flops 2216689664 | bytes 14684160 | tf_op jit(solution)/shard_map/while/body/eval_jaxpr/gld,df->glf/dot_general | solution.py:186
  821.5 75.6 %reduce-scatter.7.cloned.1.call-done = f32[256,1024]{1,0:T(8,128)} async-done(((f32[1024,1024]{1,0:T(8,128)}), f32[256,1024]{1,0:T(8,128)}) %reduce-scatter.7.cloned.1.call-update) | async-done | bytes 1048592 | tf_op jit(solution)/shard_map/while/body/eval_jaxpr/reduce_scatter | solution.py:190
  903.1 46.2 %all-gather.8.cloned.1.call-done = bf16[1,1024,1024]{2,1,0:T(8,128)(2,1)} async-done(((bf16[1,256,1024]{2,1,0:T(8,128)(2,1)}), bf16[1,1024,1024]{2,1,0:T(8,128)(2,1)}) %all-gather.8.cloned.1.call-update) | async-done | bytes 2097168 | tf_op jit(solution)/shard_map/while/body/eval_jaxpr/all_gather | solution.py:217
  963.5 75.6 %reduce-scatter.9.cloned.1.call-done = f32[256,1024]{1,0:T(8,128)} async-done(((f32[1024,1024]{1,0:T(8,128)}), f32[256,1024]{1,0:T(8,128)}) %reduce-scatter.9.cloned.1.call-update) | async-done | bytes 1048592 | tf_op jit(solution)/shard_map/while/body/eval_jaxpr/reduce_scatter | solution.py:230
  1044.8 14.0 collective-permute-done
  1062.7 12.9 collective-permute-done.1
  1086.5 8.7 fusion.240
  1095.3 11.8 multiply_reduce_fusion.18
  1107.1 12.2 multiply_convert_fusion.5
  1155.0 19.0 %reduce-scatter.11.cloned.1.call-done = bf16[256,1024]{1,0:T(8,128)(2,1)} async-done(((bf16[1024,1024]{1,0:T(8,128)(2,1)}), bf16[256,1024]{1,0:T(8,128)(2,1)}) %reduce-scatter.11.cloned.1.call-update) | async-done | bytes 524304 | tf_op jit(solution)/shard_map/while/body/eval_jaxpr/reduce_scatter | solution.py:269
  1190.9 13.8 all-reduce.1
  1205.9 40.5 %all-reduce = (f32[1024]{0:T(1024)}, f32[1024]{0:T(1024)}, f32[1024]{0:T(1024)}, f32[1024]{0:T(1024)}, f32[1024]{0:T(1024)}, /*index=5*/f32[1024]{0:T(1024)}) all-reduce(f32[1024]{0:T(1024)S(1)} %copy-done.54, f32[1024]{0:T(1024)S(1)} %copy-done.51, f32[1024]{0:T(1024)S(1)} %copy-done.48, ...), channel_id=1, replica_groups=mesh['dp'=8,'tensor'=4] {'dp','tensor'}, use_global_device_ids=true, to_apply=%region_30.31 | all-reduce | flops 6144 | bytes 49152 | tf_op jit(solution)/shard_map/psum | solution.py:370
  1246.4 48.6 %all-reduce.8.cloned.1.call-done = (bf16[3,1024,256]{2,1,0:T(8,128)(2,1)}, bf16[256,1024]{1,0:T(8,128)(2,1)}, bf16[1024,1024]{1,0:T(8,128)(2,1)}, bf16[1024,1024]{1,0:T(8,128)(2,1)}) async-done(((bf16[3,1024,256]{2,1,0:T(8,128)(2,1)}, bf16[256,1024]{1,0:T(8,128)(2,1)}, bf16[1024,1024]{1,0:T(8,128)(2,1)}, bf16[1024,1024]{1,0:T(8,128)(2,1)}), (bf16[3,1024,256]{2,1,0:T(8,128)(2,1)}, ...) | async-done | bytes 6291472 | tf_op jit(solution)/shard_map/psum | solution.py:368
  1305.6 127.1 %all-reduce.6.cloned.1.call-done = f32[1024,288]{0,1:T(8,128)} async-done(((f32[1024,288]{0,1:T(8,128)}), f32[1024,288]{0,1:T(8,128)}) %all-reduce.6.cloned.1.call-update) | async-done | bytes 1179664 | tf_op jit(solution)/shard_map/psum | solution.py:370
  (479 shorter events, 269.0 us)
Async XLA Ops:
  10.8 51.1 %all-gather.4.cloned.1.call-start = ((), (), s32[]{:S(2)}) async-start(), calls=%async_computation.6 | async-start | bytes 2621440 | tf_op jit(solution)/shard_map/while/body/eval_jaxpr/all_gather | solution.py:161
  12.7 157.6 %reduce-scatter.5.cloned.1.call-start = ((), (), s32[]{:S(2)}) async-start(), calls=%async_computation.7 | async-start | bytes 5242880 | tf_op jit(solution)/shard_map/while/body/eval_jaxpr/reduce_scatter | solution.py:171
  94.6 75.7 %copy-start.20 = (bf16[2,256,1024]{2,1,0:T(8,128)(2,1)S(1)}, bf16[2,256,1024]{2,1,0:T(8,128)(2,1)}, u32[]{:S(2)}) copy-start(bf16[2,256,1024]{2,1,0:T(8,128)(2,1)} %get-tuple-element.1248) | copy-start | bytes 3145732 | tf_op jit(solution)/shard_map/while
  94.6 75.7 %copy-start.55 = (f32[1024]{0:T(1024)S(1)}, f32[1024]{0:T(1024)}, u32[]{:S(2)}) copy-start(f32[1024]{0:T(1024)} %get-tuple-element.1252) | copy-start | bytes 12292 | tf_op jit(solution)/shard_map/while
  94.6 77.4 %copy-start.34 = (f32[1024]{0:T(1024)S(1)}, f32[1024]{0:T(1024)}, u32[]{:S(2)}) copy-start(f32[1024]{0:T(1024)} %get-tuple-element.1253) | copy-start | bytes 12292 | tf_op jit(solution)/shard_map/while
  94.6 77.4 %copy-start.35 = (f32[1024]{0:T(1024)S(1)}, f32[1024]{0:T(1024)}, u32[]{:S(2)}) copy-start(f32[1024]{0:T(1024)} %get-tuple-element.1254) | copy-start | bytes 12292 | tf_op jit(solution)/shard_map/while
  94.6 125.1 %copy-start.65 = (f32[1024]{0:T(1024)S(1)}, f32[1024]{0:T(1024)}, u32[]{:S(2)}) copy-start(f32[1024]{0:T(1024)} %get-tuple-element.1256) | copy-start | bytes 12292 | tf_op jit(solution)/shard_map/while
  94.6 125.1 %all-gather.6.cloned.1.call-start = ((), (), s32[]{:S(2)}) async-start(), calls=%async_computation.8 | async-start | bytes 2621440 | tf_op jit(solution)/shard_map/while/body/eval_jaxpr/all_gather | solution.py:184
  173.1 142.8 %reduce-scatter.7.cloned.1.call-start = ((), (), s32[]{:S(2)}) async-start(), calls=%async_computation.9 | async-start | bytes 5242880 | tf_op jit(solution)/shard_map/while/body/eval_jaxpr/reduce_scatter | solution.py:190
  240.3 77.6 %copy-start.36 = (f32[1024]{0:T(1024)S(1)}, f32[1024]{0:T(1024)}, u32[]{:S(2)}) copy-start(f32[1024]{0:T(1024)} %get-tuple-element.1262) | copy-start | bytes 12292 | tf_op jit(solution)/shard_map/while
  240.3 127.8 %all-gather.8.cloned.1.call-start = ((), (), s32[]{:S(2)}) async-start(), calls=%async_computation.10 | async-start | bytes 2621440 | tf_op jit(solution)/shard_map/while/body/eval_jaxpr/all_gather | solution.py:217
  321.5 136.5 %reduce-scatter.9.cloned.1.call-start = ((), (), s32[]{:S(2)}) async-start(), calls=%async_computation.11 | async-start | bytes 5242880 | tf_op jit(solution)/shard_map/while/body/eval_jaxpr/reduce_scatter | solution.py:230
  382.3 210.6 %reduce-scatter.11.cloned.1.call-start = ((), (), s32[]{:S(2)}) async-start(), calls=%async_computation.12 | async-start | bytes 2621440 | tf_op jit(solution)/shard_map/while/body/eval_jaxpr/reduce_scatter | solution.py:269
  462.2 15.5 %collective-permute-start = (bf16[1,256,1024]{2,1,0:T(8,128)(2,1)S(1)}, bf16[1,256,1024]{2,1,0:T(8,128)(2,1)S(1)}, u32[]{:S(2)}, u32[]{:S(2)}) collective-permute-start(bf16[1,256,1024]{2,1,0:T(8,128)(2,1)S(1)} %get-tuple-element.1114), channel_id=1, source_target_pairs={{0,1},{1,2},{2,3},{3,0},{4,5},{5,6},{6,7},{7,4},{8,9},{9,10},{10,1... | collective-permute-start | bytes 1572872 | tf_op jit(solution)/shard_map/while/body/eval_jaxpr/ppermute | solution.py:17
  477.7 16.8 %collective-permute-start.1 = (bf16[1,256,1024]{2,1,0:T(8,128)(2,1)S(1)}, bf16[1,256,1024]{2,1,0:T(8,128)(2,1)}, u32[]{:S(2)}, u32[]{:S(2)}) collective-permute-start(bf16[1,256,1024]{2,1,0:T(8,128)(2,1)S(1)} %collective-permute-done), channel_id=1, source_target_pairs={{0,1},{1,2},{2,3},{3,0},{4,5},{5,6},{6,7},{7,4},{8,9},{9,10},{10,1... | collective-permute-start | bytes 1572872 | tf_op jit(solution)/shard_map/while/body/eval_jaxpr/ppermute | solution.py:17
  477.7 24.3 %collective-permute-start.2 = (bf16[1,256,1024]{2,1,0:T(8,128)(2,1)}, bf16[1,256,1024]{2,1,0:T(8,128)(2,1)S(1)}, u32[]{:S(2)}, u32[]{:S(2)}) collective-permute-start(bf16[1,256,1024]{2,1,0:T(8,128)(2,1)} %copy-done.4), channel_id=1, source_target_pairs={{0,3},{1,0},{2,1},{3,2},{4,7},{5,4},{6,5},{7,6},{8,11},{9,8},{10,9... | collective-permute-start | bytes 1572872 | tf_op jit(solution)/shard_map/while/body/eval_jaxpr/ppermute | solution.py:19
  595.2 47.7 %all-gather.4.cloned.1.call-start = ((), (), s32[]{:S(2)}) async-start(), calls=%async_computation.6 | async-start | bytes 2621440 | tf_op jit(solution)/shard_map/while/body/eval_jaxpr/all_gather | solution.py:161
  597.2 154.2 %reduce-scatter.5.cloned.1.call-start = ((), (), s32[]{:S(2)}) async-start(), calls=%async_computation.7 | async-start | bytes 5242880 | tf_op jit(solution)/shard_map/while/body/eval_jaxpr/reduce_scatter | solution.py:171
  675.7 77.4 %copy-start.34 = (f32[1024]{0:T(1024)S(1)}, f32[1024]{0:T(1024)}, u32[]{:S(2)}) copy-start(f32[1024]{0:T(1024)} %get-tuple-element.1253) | copy-start | bytes 12292 | tf_op jit(solution)/shard_map/while
  675.7 77.4 %copy-start.35 = (f32[1024]{0:T(1024)S(1)}, f32[1024]{0:T(1024)}, u32[]{:S(2)}) copy-start(f32[1024]{0:T(1024)} %get-tuple-element.1254) | copy-start | bytes 12292 | tf_op jit(solution)/shard_map/while
  675.7 125.1 %copy-start.65 = (f32[1024]{0:T(1024)S(1)}, f32[1024]{0:T(1024)}, u32[]{:S(2)}) copy-start(f32[1024]{0:T(1024)} %get-tuple-element.1256) | copy-start | bytes 12292 | tf_op jit(solution)/shard_map/while
  675.8 125.1 %all-gather.6.cloned.1.call-start = ((), (), s32[]{:S(2)}) async-start(), calls=%async_computation.8 | async-start | bytes 2621440 | tf_op jit(solution)/shard_map/while/body/eval_jaxpr/all_gather | solution.py:184
  754.2 142.8 %reduce-scatter.7.cloned.1.call-start = ((), (), s32[]{:S(2)}) async-start(), calls=%async_computation.9 | async-start | bytes 5242880 | tf_op jit(solution)/shard_map/while/body/eval_jaxpr/reduce_scatter | solution.py:190
  821.4 77.6 %copy-start.36 = (f32[1024]{0:T(1024)S(1)}, f32[1024]{0:T(1024)}, u32[]{:S(2)}) copy-start(f32[1024]{0:T(1024)} %get-tuple-element.1262) | copy-start | bytes 12292 | tf_op jit(solution)/shard_map/while
  821.4 127.8 %all-gather.8.cloned.1.call-start = ((), (), s32[]{:S(2)}) async-start(), calls=%async_computation.10 | async-start | bytes 2621440 | tf_op jit(solution)/shard_map/while/body/eval_jaxpr/all_gather | solution.py:217
  902.7 136.4 %reduce-scatter.9.cloned.1.call-start = ((), (), s32[]{:S(2)}) async-start(), calls=%async_computation.11 | async-start | bytes 5242880 | tf_op jit(solution)/shard_map/while/body/eval_jaxpr/reduce_scatter | solution.py:230
  963.5 210.6 %reduce-scatter.11.cloned.1.call-start = ((), (), s32[]{:S(2)}) async-start(), calls=%async_computation.12 | async-start | bytes 2621440 | tf_op jit(solution)/shard_map/while/body/eval_jaxpr/reduce_scatter | solution.py:269
  1043.3 15.5 %collective-permute-start = (bf16[1,256,1024]{2,1,0:T(8,128)(2,1)S(1)}, bf16[1,256,1024]{2,1,0:T(8,128)(2,1)S(1)}, u32[]{:S(2)}, u32[]{:S(2)}) collective-permute-start(bf16[1,256,1024]{2,1,0:T(8,128)(2,1)S(1)} %get-tuple-element.1114), channel_id=1, source_target_pairs={{0,1},{1,2},{2,3},{3,0},{4,5},{5,6},{6,7},{7,4},{8,9},{9,10},{10,1... | collective-permute-start | bytes 1572872 | tf_op jit(solution)/shard_map/while/body/eval_jaxpr/ppermute | solution.py:17
  1058.8 16.8 %collective-permute-start.1 = (bf16[1,256,1024]{2,1,0:T(8,128)(2,1)S(1)}, bf16[1,256,1024]{2,1,0:T(8,128)(2,1)}, u32[]{:S(2)}, u32[]{:S(2)}) collective-permute-start(bf16[1,256,1024]{2,1,0:T(8,128)(2,1)S(1)} %collective-permute-done), channel_id=1, source_target_pairs={{0,1},{1,2},{2,3},{3,0},{4,5},{5,6},{6,7},{7,4},{8,9},{9,10},{10,1... | collective-permute-start | bytes 1572872 | tf_op jit(solution)/shard_map/while/body/eval_jaxpr/ppermute | solution.py:17
  1058.9 24.3 %collective-permute-start.2 = (bf16[1,256,1024]{2,1,0:T(8,128)(2,1)}, bf16[1,256,1024]{2,1,0:T(8,128)(2,1)S(1)}, u32[]{:S(2)}, u32[]{:S(2)}) collective-permute-start(bf16[1,256,1024]{2,1,0:T(8,128)(2,1)} %copy-done.4), channel_id=1, source_target_pairs={{0,3},{1,0},{2,1},{3,2},{4,7},{5,4},{6,5},{7,6},{8,11},{9,8},{10,9... | collective-permute-start | bytes 1572872 | tf_op jit(solution)/shard_map/while/body/eval_jaxpr/ppermute | solution.py:19
  1179.3 115.7 %all-reduce.8.cloned.1.call-start = ((), (), s32[]{:S(2)}) async-start(), calls=%async_computation.5 | async-start | bytes 12582912 | tf_op jit(solution)/shard_map/psum | solution.py:368
  1190.3 242.5 %all-reduce.6.cloned.1.call-start = ((), (), s32[]{:S(2)}) async-start(), calls=%async_computation.4 | async-start | bytes 2359296 | tf_op jit(solution)/shard_map/psum | solution.py:370
  (119 other events, 1139.5 us)
Sparse Core Ops, SparseCore 0:
  13.2 48.6 all-gather.3
  94.8 75.4 reduce-scatter.4
  173.2 46.4 all-gather.5
  240.4 75.4 reduce-scatter.6
  321.6 46.4 all-gather.7
  382.5 75.4 reduce-scatter.8
  549.3 43.5 reduce-scatter.10
  597.7 45.2 all-gather.3
  675.9 75.4 reduce-scatter.4
  754.3 46.4 all-gather.5
  821.6 75.4 reduce-scatter.6
  902.8 46.4 all-gather.7
  963.6 75.4 reduce-scatter.8
  1130.4 43.5 reduce-scatter.10
Sparse Core Ops, SparseCore 1:
  1190.4 104.6 all-reduce.7
  1301.7 130.9 all-reduce.5
